TPU v7x, 256 devices: a whole 4x4x8 slice. The times are simulated.
256 devices in a mesh: roll: 4 (over z_lo, core), mach: 16 (over y, x), cross: 4 (over z_hi).
Axes of the slice: x: 4, y: 4, z: 8 (z_hi: 4, z_lo: 2; z = z_hi * 2 + z_lo), core: 2. Of those that a mesh axis runs over, the one named last changes fastest.
Arguments:
- density: bfloat16 [128, 4096, 2048], P('roll', 'mach', 'cross'), may hold values from 0 to 1
- roll_start: float32 [32, 128], P(None, 'roll'), may hold values from 0.05 to 1
- mach_factor: bfloat16 [32, 4096], P(None, 'mach'), may hold values from 0.0099487305 to 1
- cross_factor: bfloat16 [32, 2048], P(None, 'cross'), may hold values from 0.0099487305 to 1
Outputs:
- roll_factor: float32 [32, 128], P(None, 'roll')
- mode_two: float32 [32, 4096], P(None, ('mach', 'cross'))
All inputs are finite; a program needn't handle non-finite values.
Results may differ from a plain program's by a relative error of at most 0.0003.
Values sent between devices are 32-bit elements; how exact they have to be, the bound alone decides.
A program may use at most 64 MiB of HBM per device.

v0:
```python
import jax
import jax.numpy as jnp
from jax import lax
from jax.sharding import PartitionSpec as P


def hals_rows(roll_rows, mttkrp, gram):

    def column_step(column, rows):
        column = jnp.asarray(column).astype(jnp.int32)
        gram_row = lax.dynamic_slice_in_dim(gram, column, 1, 0)
        diag_entry = lax.dynamic_slice_in_dim(gram_row, column, 1, 1)
        current = lax.dynamic_slice_in_dim(rows, column, 1, 0)
        target = lax.dynamic_slice_in_dim(mttkrp, column, 1, 0)
        mixed = jnp.dot(gram_row, rows, precision=lax.Precision.HIGHEST)
        updated = jnp.maximum(current + (target - mixed) / diag_entry, 0.0)
        return lax.dynamic_update_slice_in_dim(rows, updated, column, 0)

    return lax.fori_loop(0, roll_rows.shape[0], column_step, roll_rows)


def local(density, roll_start, mach_factor, cross_factor):
    rolls_here, bins_here, cross_here = density.shape
    rank = cross_factor.shape[0]
    flat = density.reshape(rolls_here * bins_here, cross_here)
    partial_value = lax.dot_general(
        cross_factor, flat, (((1,), (1,)), ((), ())), preferred_element_type=jnp.float32
    )
    partial_value = partial_value.reshape(rank, rolls_here, bins_here)
    local_terms = jnp.einsum(
        "rij,rj->ri",
        partial_value,
        mach_factor.astype(jnp.float32),
        precision=lax.Precision.HIGHEST,
    )
    local_mach = jnp.dot(mach_factor, mach_factor.T, preferred_element_type=jnp.float32)
    local_cross = jnp.dot(cross_factor, cross_factor.T, preferred_element_type=jnp.float32)
    a = lax.axis_index("roll")
    m = lax.axis_index("mach")
    c = lax.axis_index("cross")
    nroll = lax.axis_size("roll")
    slots = jnp.zeros((nroll + 2, rank, rank), jnp.float32)
    slots = lax.dynamic_update_slice_in_dim(slots, local_terms[None], a, 0)
    slots = slots.at[nroll].set(jnp.where((a == 0) & (c == 0), local_mach, 0.0))
    slots = slots.at[nroll + 1].set(jnp.where((a == 0) & (m == 0), local_cross, 0.0))
    tot = lax.psum(slots, ("roll", "mach", "cross"))
    mttkrp = lax.dynamic_index_in_dim(tot, a, 0, keepdims=False)
    gram = tot[nroll] * tot[nroll + 1]
    roll_factor = hals_rows(roll_start, mttkrp, gram)
    term = jnp.einsum("rij,ri->rj", partial_value, roll_factor, precision=lax.Precision.HIGHEST)
    nm = lax.axis_size("mach")
    ms = jnp.zeros((nm,) + term.shape, jnp.float32)
    ms = lax.dynamic_update_slice_in_dim(ms, term[None], m, 0)
    whole = lax.psum(ms, ("roll", "mach", "cross"))
    whole = lax.dynamic_index_in_dim(whole, m, 0, keepdims=False)
    span = whole.shape[1] // lax.axis_size("cross")
    total = lax.dynamic_slice_in_dim(whole, c * span, span, 1)
    scale = rank / (rolls_here * nroll * cross_here * lax.axis_size("cross"))
    return (roll_factor, total * scale)


def solution(mesh):
    in_specs = (P("roll", "mach", "cross"), P(None, "roll"), P(None, "mach"), P(None, "cross"))
    out_specs = (P(None, "roll"), P(None, ("mach", "cross")))
    return jax.shard_map(local, mesh=mesh, in_specs=in_specs, out_specs=out_specs, check_vma=False)
```

profile of v0, /device:TPU:2, one launch (start us, length us, event | category | flops | bytes accessed | tf_op | source)
XLA Modules:
  0.0 399.3 jit_solution(10247666444916578830)
XLA Ops:
  7.3 0.7 copy-done
  7.9 5.9 %fusion.13 = f32[32,32,256]{2,0,1:T(8,128)S(1)} fusion(bf16[32,256,512]{2,1,0:T(8,128)(2,1)} %param.10, bf16[32,512]{1,0:T(8,128)(2,1)S(1)} %copy-done), kind=kOutput, calls=%fused_computation.19 | convolution fusion | flops 268435456 | bytes 9469952 | tf_op jit(solution)/shard_map/dot_general | solution.py:26
  13.8 1.2 fusion.11
  15.3 79.2 %psum.14 = f32[6,32,32]{2,1,0:T(8,128)S(1)} all-reduce(f32[6,32,32]{2,1,0:T(8,128)S(1)} %fusion.6), channel_id=1, replica_groups=mesh['roll'=4,'mach'=16,'cross'=4] {'roll','mach','cross'}, use_global_device_ids=true, to_apply=%region_0.1 | all-reduce | flops 6144 | bytes 49152 | tf_op jit(solution)/shard_map/psum | solution.py:46
  94.5 45.2 %while.18 = (s32[]{:T(128)}, f32[32,32]{1,0:T(8,128)S(1)}, f32[32,32]{1,0:T(8,128)S(1)}, f32[32,32]{1,0:T(8,128)S(1)}, s32[]{:T(128)}, /*index=5*/s32[]{:T(128)}, s32[]{:T(128)}) while((s32[]{:T(128)}, f32[32,32]{1,0:T(8,128)S(1)}, f32[32,32]{1,0:T(8,128)S(1)}, f32[32,32]{1,0:T(8,128)S(1)}, s32[]{:T(128)}, /*index=5*/s32[]{:T(128)}, ...), condition=%wide.region_2.3_spmd, body=%wide.region_1.2_spmd.sunk | while | flops 12419 | bytes 19949 | solution.py:19
  94.5 0.6 dynamic_slice.74
  95.1 0.8 fusion.29
  95.9 0.6 dynamic_slice.74
  96.5 0.8 fusion.29
  97.3 0.6 dynamic_slice.74
  97.9 0.8 fusion.29
  98.8 0.6 dynamic_slice.74
  99.3 0.8 fusion.29
  100.2 0.6 dynamic_slice.74
  100.8 0.8 fusion.29
  101.6 0.6 dynamic_slice.74
  102.2 0.8 fusion.29
  103.0 0.6 dynamic_slice.74
  103.6 0.8 fusion.29
  104.4 0.6 dynamic_slice.74
  105.0 0.8 fusion.29
  105.8 0.6 dynamic_slice.74
  106.4 0.8 fusion.29
  107.2 0.6 dynamic_slice.74
  107.8 0.8 fusion.29
  108.6 0.6 dynamic_slice.74
  109.2 0.8 fusion.29
  110.1 0.6 dynamic_slice.74
  110.6 0.8 fusion.29
  111.5 0.6 dynamic_slice.74
  112.1 0.8 fusion.29
  112.9 0.6 dynamic_slice.74
  113.5 0.8 fusion.29
  114.3 0.6 dynamic_slice.74
  114.9 0.8 fusion.29
  115.7 0.6 dynamic_slice.74
  116.3 0.8 fusion.29
  117.1 0.6 dynamic_slice.74
  117.7 0.8 fusion.29
  118.5 0.6 dynamic_slice.74
  119.1 0.8 fusion.29
  119.9 0.6 dynamic_slice.74
  120.5 0.8 fusion.29
  121.3 0.6 dynamic_slice.74
  121.9 0.8 fusion.29
  122.8 0.6 dynamic_slice.74
  123.3 0.8 fusion.29
  124.2 0.6 dynamic_slice.74
  124.8 0.8 fusion.29
  126.2 0.8 fusion.29
  127.6 0.8 fusion.29
  129.0 0.8 fusion.29
  130.4 0.8 fusion.29
  131.8 0.8 fusion.29
  133.2 0.8 fusion.29
  134.6 0.8 fusion.29
  135.5 0.6 dynamic_slice.74
  136.0 0.8 fusion.29
  137.5 0.8 fusion.29
  138.9 0.8 fusion.29
  139.7 1.3 fusion.9
  141.0 0.8 copy-done.1
  141.9 249.1 %all-reduce.2.cloned.1.call-done = f32[16,32,256]{2,1,0:T(8,128)} async-done(((f32[16,32,256]{2,1,0:T(8,128)}), f32[16,32,256]{2,1,0:T(8,128)}) %all-reduce.2.cloned.1.call-update) | async-done | bytes 524304 | tf_op jit(solution)/shard_map/psum | solution.py:54
  391.0 1.4 multiply_bitcast_fusion
  (58 shorter events, 6.5 us)
Async XLA Ops:
  7.2 0.8 copy-start
  7.2 6.7 %copy-start.4 = (bf16[32,256]{1,0:T(8,128)(2,1)S(1)}, bf16[32,256]{1,0:T(8,128)(2,1)}, u32[]{:S(2)}) copy-start(bf16[32,256]{1,0:T(8,128)(2,1)} %param.12) | copy-start | bytes 49156
  7.2 87.3 %copy-start.3 = (f32[32,32]{1,0:T(8,128)S(1)}, f32[32,32]{1,0:T(8,128)}, u32[]{:S(2)}) copy-start(f32[32,32]{1,0:T(8,128)} %param.11) | copy-start | bytes 12292
  7.2 383.8 %all-reduce.2.cloned.1.call-start = ((), (), s32[]{:S(2)}) async-start(), calls=%async_computation | async-start | bytes 1048576 | tf_op jit(solution)/shard_map/psum | solution.py:54
  139.7 252.8 %copy-start.2 = (f32[32,32]{1,0:T(8,128)}, f32[32,32]{1,0:T(8,128)S(1)}, u32[]{:S(2)}) copy-start(f32[32,32]{1,0:T(8,128)S(1)} %get-tuple-element.148) | copy-start | bytes 12292
  141.0 0.8 copy-start.1
Sparse Core Ops, SparseCore 0:
  142.0 248.9 all-reduce.1
where the time goes:
time: 400 us; the launch traced here: 399 us
  waiting for transfers between devices  249 us (62%)
  blocking collectives  79.2 us (20%)
  matrix products  33.6 us (8%)
  local copies, waits for them, and re-layouts  21.2 us (5%)
  between operations  14.2 us (4%)
    psum x1, waiting for transfers between devices, local(): whole = lax.psum(ms, ('roll', 'mach', 'cross'))  249 us
    psum x1, blocking collectives, local(): tot = lax.psum(slots, ('roll', 'mach', 'cross'))  79.2 us
    dot_general x32, matrix products, column_step(): mixed = jnp.dot(gram_row, rows, precision=lax.Precision.HIGHEST)  25 us
    dynamic_slice x32, local copies, waits for them, and re-layouts, column_step(): diag_entry = lax.dynamic_slice_in_dim(gram_row, column, 1, 1)  18.8 us
  transfers between devices with their start and end apart: 1, of which 1 were waited for; matrix products, arithmetic and copies ran while one was open for 0% of the time, Pallas kernels for 0%

commit v1 on v0

--- a/solution.py
+++ b/solution.py
@@ -51,7 +51,8 @@
     nm = lax.axis_size("mach")
     ms = jnp.zeros((nm,) + term.shape, jnp.float32)
     ms = lax.dynamic_update_slice_in_dim(ms, term[None], m, 0)
-    whole = lax.psum(ms, ("roll", "mach", "cross"))
+    one_axis = lax.psum(ms, ("mach", "cross"))
+    whole = lax.psum(one_axis, "roll")
     whole = lax.dynamic_index_in_dim(whole, m, 0, keepdims=False)
     span = whole.shape[1] // lax.axis_size("cross")
     total = lax.dynamic_slice_in_dim(whole, c * span, span, 1)

time: 400 us -> 921 us (2.30)
  waiting for transfers between devices: 249 us -> 768 us
    psum x1 -> x2, waiting for transfers between devices: 249 us -> 768 us  [the longest x1 721 us: local(): one_axis = lax.psum(ms, ('mach', 'cross'))]
  transfers between devices with their start and end apart: 1 -> 2, of which waited for: 1 -> 2; matrix products, arithmetic and copies ran while one was open for 0% -> 0% of each run, Pallas kernels for 0% -> 0%
where the time goes in v1:
time: 921 us; the launch traced here: 919 us
  waiting for transfers between devices  768 us (83%)
  blocking collectives  79.2 us (9%)
  matrix products  33.6 us (4%)
  local copies, waits for them, and re-layouts  21.2 us (2%)
  between operations  14.2 us (2%)
    psum x1, waiting for transfers between devices, local(): one_axis = lax.psum(ms, ('mach', 'cross'))  721 us
    psum x1, blocking collectives, local(): tot = lax.psum(slots, ('roll', 'mach', 'cross'))  79.2 us
    psum x1, waiting for transfers between devices, local(): whole = lax.psum(one_axis, 'roll')  47.2 us
    dot_general x32, matrix products, column_step(): mixed = jnp.dot(gram_row, rows, precision=lax.Precision.HIGHEST)  25 us
    dynamic_slice x32, local copies, waits for them, and re-layouts, column_step(): diag_entry = lax.dynamic_slice_in_dim(gram_row, column, 1, 1)  18.8 us
  transfers between devices with their start and end apart: 2, of which 2 were waited for; matrix products, arithmetic and copies ran while one was open for 0% of the time, Pallas kernels for 0%

profile of v1, /device:TPU:2, one launch (start us, length us, event | category | flops | bytes accessed | tf_op | source)
XLA Modules:
  0.0 918.6 jit_solution(9907768711191541369)
XLA Ops:
  7.3 0.7 copy-done
  7.9 5.9 fusion.13
  13.8 1.2 fusion.11
  15.3 79.2 %psum.21 = f32[6,32,32]{2,1,0:T(8,128)S(1)} all-reduce(f32[6,32,32]{2,1,0:T(8,128)S(1)} %fusion.6), channel_id=1, replica_groups=mesh['roll'=4,'mach'=16,'cross'=4] {'roll','mach','cross'}, use_global_device_ids=true, to_apply=%region_0.1 | all-reduce | flops 6144 | bytes 49152 | tf_op jit(solution)/shard_map/psum | solution.py:46
  94.5 45.2 %while.18 = (s32[]{:T(128)}, f32[32,32]{1,0:T(8,128)S(1)}, f32[32,32]{1,0:T(8,128)S(1)}, f32[32,32]{1,0:T(8,128)S(1)}, s32[]{:T(128)}, /*index=5*/s32[]{:T(128)}, s32[]{:T(128)}) while((s32[]{:T(128)}, f32[32,32]{1,0:T(8,128)S(1)}, f32[32,32]{1,0:T(8,128)S(1)}, f32[32,32]{1,0:T(8,128)S(1)}, s32[]{:T(128)}, /*index=5*/s32[]{:T(128)}, ...), condition=%wide.region_2.3_spmd, body=%wide.region_1.2_spmd.sunk | while | flops 12419 | bytes 19949 | solution.py:19
  94.5 0.6 dynamic_slice.74
  95.1 0.8 fusion.29
  95.9 0.6 dynamic_slice.74
  96.5 0.8 fusion.29
  97.4 0.6 dynamic_slice.74
  97.9 0.8 fusion.29
  98.8 0.6 dynamic_slice.74
  99.4 0.8 fusion.29
  100.2 0.6 dynamic_slice.74
  100.8 0.8 fusion.29
  101.6 0.6 dynamic_slice.74
  102.2 0.8 fusion.29
  103.0 0.6 dynamic_slice.74
  103.6 0.8 fusion.29
  104.4 0.6 dynamic_slice.74
  105.0 0.8 fusion.29
  105.8 0.6 dynamic_slice.74
  106.4 0.8 fusion.29
  107.2 0.6 dynamic_slice.74
  107.8 0.8 fusion.29
  108.6 0.6 dynamic_slice.74
  109.2 0.8 fusion.29
  110.1 0.6 dynamic_slice.74
  110.6 0.8 fusion.29
  111.5 0.6 dynamic_slice.74
  112.1 0.8 fusion.29
  112.9 0.6 dynamic_slice.74
  113.5 0.8 fusion.29
  114.3 0.6 dynamic_slice.74
  114.9 0.8 fusion.29
  115.7 0.6 dynamic_slice.74
  116.3 0.8 fusion.29
  117.1 0.6 dynamic_slice.74
  117.7 0.8 fusion.29
  118.5 0.6 dynamic_slice.74
  119.1 0.8 fusion.29
  119.9 0.6 dynamic_slice.74
  120.5 0.8 fusion.29
  121.3 0.6 dynamic_slice.74
  121.9 0.8 fusion.29
  122.8 0.6 dynamic_slice.74
  123.3 0.8 fusion.29
  124.2 0.6 dynamic_slice.74
  124.8 0.8 fusion.29
  126.2 0.8 fusion.29
  127.6 0.8 fusion.29
  129.0 0.8 fusion.29
  130.4 0.8 fusion.29
  131.8 0.8 fusion.29
  133.2 0.8 fusion.29
  134.6 0.8 fusion.29
  136.1 0.8 fusion.29
  137.5 0.8 fusion.29
  138.9 0.8 fusion.29
  139.7 1.3 fusion.9
  141.0 0.8 copy-done.1
  141.9 721.2 %all-reduce.3.cloned.1.call-done = f32[16,32,256]{2,1,0:T(8,128)} async-done(((f32[16,32,256]{2,1,0:T(8,128)}), f32[16,32,256]{2,1,0:T(8,128)}) %all-reduce.3.cloned.1.call-update) | async-done | bytes 524304 | tf_op jit(solution)/shard_map/psum | solution.py:54
  863.1 47.2 %all-reduce.5.cloned.1.call-done = f32[16,32,256]{2,1,0:T(8,128)} async-done(((f32[16,32,256]{2,1,0:T(8,128)}), f32[16,32,256]{2,1,0:T(8,128)}) %all-reduce.5.cloned.1.call-update) | async-done | bytes 524304 | tf_op jit(solution)/shard_map/psum | solution.py:55
  910.3 1.4 multiply_bitcast_fusion
  (61 shorter events, 7.2 us)
Async XLA Ops:
  7.2 0.8 copy-start
  7.2 6.7 copy-start.4
  7.2 87.3 %copy-start.3 = (f32[32,32]{1,0:T(8,128)S(1)}, f32[32,32]{1,0:T(8,128)}, u32[]{:S(2)}) copy-start(f32[32,32]{1,0:T(8,128)} %param.11) | copy-start | bytes 12292
  7.2 855.9 %all-reduce.3.cloned.1.call-start = ((), (), s32[]{:S(2)}) async-start(), calls=%async_computation | async-start | bytes 1048576 | tf_op jit(solution)/shard_map/psum | solution.py:54
  139.7 772.1 %copy-start.2 = (f32[32,32]{1,0:T(8,128)}, f32[32,32]{1,0:T(8,128)S(1)}, u32[]{:S(2)}) copy-start(f32[32,32]{1,0:T(8,128)S(1)} %get-tuple-element.148) | copy-start | bytes 12292
  141.0 0.8 copy-start.1
  141.9 768.4 %all-reduce.5.cloned.1.call-start = ((), (), s32[]{:S(2)}) async-start(), calls=%async_computation.1 | async-start | bytes 1048576 | tf_op jit(solution)/shard_map/psum | solution.py:55
Sparse Core Ops, SparseCore 0:
  142.0 721.0 all-reduce.2
  865.9 44.3 all-reduce.4
